TPU v7x, 1024 devices: a whole 4x4x32 slice. The times are simulated.
1024 devices in a mesh: section: 8 (over x, core), expert: 32 (over y, z_lo), replica: 4 (over z_hi).
Axes of the slice: x: 4, y: 4, z: 32 (z_hi: 4, z_lo: 8; z = z_hi * 8 + z_lo), core: 2. Of those that a mesh axis runs over, the one named last changes fastest.
Arguments:
- token_grads: bfloat16 [8, 2048, 3584], P('section', 'expert', 'replica'), may hold values from -6 to 6
- routing: int32 [8, 2048, 4], P('section', 'expert'), may hold values from 0 to 7, all different within a row; in each aligned block of 64 rows (0 to 63, 64 to 127, ..., all dimensions but the last counted through in order) at most 34 rows name the same one
- gate_weights: float32 [8, 2048, 4], P('section', 'expert'), may hold values from 0.1 to 1
- layer_inputs: bfloat16 [8, 2048, 3584], P('section', 'expert', 'replica'), may hold values from -6 to 6
- w_gate: bfloat16 [8, 3584, 8192], P('section', 'replica', 'expert'), may hold values from -0.09375 to 0.09375
- w_up: bfloat16 [8, 3584, 8192], P('section', 'replica', 'expert'), may hold values from -0.09375 to 0.09375
- w_down: bfloat16 [8, 3584, 8192], P('section', 'replica', 'expert'), may hold values from -0.09375 to 0.09375
Outputs:
- upstream: bfloat16 [8, 2048, 3584], P('section', 'expert', 'replica')
- grad_gate: bfloat16 [8, 3584, 8192], P('section', 'replica', 'expert')
- grad_up: bfloat16 [8, 3584, 8192], P('section', 'replica', 'expert')
- grad_down: bfloat16 [8, 3584, 8192], P('section', 'replica', 'expert')
Inputs may be any that keep to these rules, and one draw needn't show every extreme that they name: `routing`: each token names 4 different experts. Among the 64 tokens of one group no expert is named more than 34 times, and in every draw some group names some expert exactly 34 times.
All inputs are finite; a program needn't handle non-finite values.
Results may differ from a plain program's by a relative error of at most 0.0064.
Values may be sent and summed in bfloat16 or wider, within the bound.
A program may use at most 32 MiB of HBM per device.

v0:
```python
import jax
import jax.numpy as jnp
from jax import lax
from jax.sharding import PartitionSpec as P

SHARES = 4


def in_one_piece(arrays, axis, split_dim, concat_dim, along):
    ends, at = ([], 0)
    for a in arrays[:-1]:
        at += a.shape[along]
        ends.append(at)
    both = jnp.concatenate(arrays, axis=along)
    return tuple(
        jnp.split(
            lax.all_to_all(both, axis, split_axis=split_dim, concat_axis=concat_dim, tiled=True),
            ends,
            axis=along,
        )
    )


def in_one_piece_2(arrays, axis, dim, along):
    both = jnp.concatenate(arrays, axis=along)
    filled, at, finished = (lax.psum_scatter(both, axis, scatter_dimension=dim, tiled=True), 0, [])
    for a in arrays:
        finished.append(lax.slice_in_dim(filled, at, at + a.shape[along], axis=along))
        at += a.shape[along]
    return tuple(finished)


def side_by_side(arrays, axis, dim, along):
    ends, at = ([], 0)
    for a in arrays[:-1]:
        at += a.shape[along]
        ends.append(at)
    both = jnp.concatenate(arrays, axis=along)
    return tuple(jnp.split(lax.all_gather(both, axis, axis=dim, tiled=True), ends, axis=along))


def shifted(value, axis, steps):
    count = lax.axis_size(axis)
    first, last = (max(0, -steps), min(count, count - steps))
    return lax.ppermute(value, axis, [(source, source + steps) for source in range(first, last)])


def slot_index(routes, n_experts, capacity):
    flat_route = routes.reshape(-1)
    one_hot = (flat_route[:, None] == jnp.arange(n_experts, dtype=jnp.int32)[None, :]).astype(
        jnp.int32
    )
    before = jnp.cumsum(one_hot, axis=0) - one_hot
    rank_in = jnp.sum(before * one_hot, axis=1)
    return flat_route * capacity + rank_in


def dispatch_rows(grad_rows, routes, weights, n_experts, capacity):
    feature_width = grad_rows.shape[1]
    scaled = (grad_rows.astype(jnp.float32)[:, None, :] * weights[:, :, None]).reshape(
        -1, feature_width
    )
    positions = slot_index(routes, n_experts, capacity)
    blank_rows = jnp.zeros((n_experts * capacity, feature_width), jnp.float32)
    return blank_rows.at[positions].set(scaled).astype(jnp.bfloat16)


def place_rows(inputs, routes, n_experts, capacity):
    feature_width = inputs.shape[1]
    chosen = routes.shape[1]
    copies = jnp.broadcast_to(inputs[:, None, :], (inputs.shape[0], chosen, feature_width)).reshape(
        -1, feature_width
    )
    positions = slot_index(routes, n_experts, capacity)
    blank_rows = jnp.zeros((n_experts * capacity, feature_width), inputs.dtype)
    return blank_rows.at[positions].set(copies)


def activations(gate_pre, up_pre, grad_hidden):
    sigmoid_gate = jax.nn.sigmoid(gate_pre)
    activated = gate_pre * sigmoid_gate
    hidden = (activated * up_pre).astype(jnp.bfloat16)
    slope_term = sigmoid_gate * (1.0 + gate_pre * (1.0 - sigmoid_gate))
    d_gate = (grad_hidden * up_pre * slope_term).astype(jnp.bfloat16)
    d_up = (grad_hidden * activated).astype(jnp.bfloat16)
    return (hidden, d_gate, d_up)


def contract_rows(left, right):
    return lax.dot_general(
        left, right, (((0,), (0,)), ((), ())), preferred_element_type=jnp.float32
    )


def contract_cols(left, right):
    return lax.dot_general(
        left, right, (((1,), (1,)), ((), ())), preferred_element_type=jnp.float32
    )


def per_device(token_grads, routing, gate_weights, layer_inputs, w_gate, w_up, w_down):
    n_groups = lax.axis_size("expert")
    n_experts = n_groups // SHARES
    grad_rows = token_grads[0]
    routes = routing[0]
    weights = gate_weights[0]
    inputs = layer_inputs[0]
    gate_cols = w_gate[0]
    up_cols = w_up[0]
    down_cols = w_down[0]
    n_tokens = routes.shape[0]
    chosen = routes.shape[1]
    columns = grad_rows.shape[1]
    capacity = min(n_tokens, 17 * n_tokens * chosen // (16 * n_experts))
    outgoing = dispatch_rows(grad_rows, routes, weights, n_experts, capacity).reshape(
        n_experts, capacity, columns
    )
    outgoing = jnp.repeat(outgoing, SHARES, axis=0)
    placed = place_rows(inputs, routes, n_experts, capacity).reshape(n_experts, capacity, columns)
    placed = jnp.repeat(placed, SHARES, axis=0)
    received, saved = in_one_piece((outgoing, placed), "expert", 0, 0, 1)
    received = received.reshape(n_groups * capacity, columns)
    saved = saved.reshape(n_groups * capacity, columns)
    gate_part = jnp.dot(saved, gate_cols, preferred_element_type=jnp.float32)
    up_part = jnp.dot(saved, up_cols, preferred_element_type=jnp.float32)
    down_part = jnp.dot(received, down_cols, preferred_element_type=jnp.float32)
    gate_share, up_share, grad_share = in_one_piece_2(
        (gate_part, up_part, down_part), "replica", 0, 1
    )
    hidden_share, d_gate_share, d_up_share = activations(gate_share, up_share, grad_share)
    hidden, d_gate, d_up = side_by_side((hidden_share, d_gate_share, d_up_share), "replica", 0, 1)
    back_rows = (contract_cols(d_gate, gate_cols) + contract_cols(d_up, up_cols)).astype(
        jnp.bfloat16
    )
    returned = lax.all_to_all(
        back_rows.reshape(n_groups, capacity, columns),
        "expert",
        split_axis=0,
        concat_axis=0,
        tiled=True,
    )
    merged = jnp.sum(
        returned.reshape(n_experts, SHARES, capacity, columns).astype(jnp.float32), axis=1
    )
    merged = merged.reshape(n_experts * capacity, columns)
    positions = slot_index(routes, n_experts, capacity)
    picked = merged[positions].reshape(n_tokens, chosen, columns)
    boundary = jnp.sum(picked, axis=1).astype(jnp.bfloat16)
    upstream = shifted(boundary[None], "section", -1)
    grad_gate = contract_rows(saved, d_gate).astype(jnp.bfloat16)
    grad_up = contract_rows(saved, d_up).astype(jnp.bfloat16)
    grad_down = contract_rows(received, hidden).astype(jnp.bfloat16)
    return (upstream, grad_gate[None], grad_up[None], grad_down[None])


def solution(mesh):
    placed = (
        P("section", "expert", "replica"),
        P("section", "expert", None),
        P("section", "expert", None),
        P("section", "expert", "replica"),
        P("section", "replica", "expert"),
        P("section", "replica", "expert"),
        P("section", "replica", "expert"),
    )
    return jax.shard_map(
        per_device,
        mesh=mesh,
        in_specs=placed,
        out_specs=(
            P("section", "expert", "replica"),
            P("section", "replica", "expert"),
            P("section", "replica", "expert"),
            P("section", "replica", "expert"),
        ),
        check_vma=False,
    )
```

profile of v0, /device:TPU:43, one launch (start us, length us, event | category | flops | bytes accessed | tf_op | source)
XLA Modules:
  0.0 780.2 jit_solution(991582465215456343)
XLA Ops:
  7.2 0.0 copy-start
  7.2 0.0 copy-start.4
  7.2 0.0 reduce-scatter.2.cloned.1.call-start
  7.2 0.8 copy.12
  8.1 0.1 eq.43
  8.2 0.1 eq.18
  8.3 0.7 broadcast_multiply_fusion
  9.0 0.6 reduce-window.6
  9.5 0.2 slice_reduce_fusion
  9.8 0.1 copy.11
  9.9 0.1 mul.60
  10.0 0.9 bitcast_convert_fusion
  10.9 0.2 mul.62
  11.1 0.3 mul.63
  11.4 0.0 copy-done.4
  11.4 0.1 copy.14
  11.5 0.1 mul.64
  11.6 0.1 fusion.26
  11.7 0.0 copy-start.3
  11.7 1.8 scatter_custom_fusion
  13.5 0.1 convert_element_type.66
  13.6 0.1 reshape.108
  13.7 0.1 broadcast_in_dim.40
  13.9 0.1 reshape.140
  14.0 1.8 scatter_custom_fusion.1
  15.8 0.1 reshape.111
  15.9 0.2 broadcast_in_dim.37
  16.1 0.2 broadcast_in_dim.41
  16.3 1.1 pad_maximum_fusion
  17.4 196.7 %all_to_all.10 = bf16[32,68,896]{2,1,0:T(8,128)(2,1)S(1)} all-to-all(bf16[32,68,896]{2,1,0:T(8,128)(2,1)S(1)} %pad_maximum_fusion), channel_id=1, replica_groups=mesh['section'=8,'expert'=32,'replica'=4] {'expert'}, dimensions={0} | all-to-all | bytes 7798784 | tf_op jit(solution)/shard_map/all_to_all | solution.py:17
  214.1 3.0 fusion.28
  217.1 2.6 reshape.113
  219.7 1.8 fusion.16
  221.5 0.0 copy-done
  221.5 1.7 fusion.19
  223.2 4.0 reshape.114
  227.3 2.4 fusion.13
  229.7 0.0 copy-done.1
  229.7 1.9 pad_maximum_fusion.1
  231.6 0.0 reduce-scatter.2.cloned.1.call-update
  231.6 0.0 all-gather.2.cloned.1.call-start
  231.7 254.7 %reduce-scatter.2.cloned.1.call-done = f32[272,768]{1,0:T(8,128)} async-done(((f32[1088,768]{1,0:T(8,128)}), f32[272,768]{1,0:T(8,128)}) %reduce-scatter.2.cloned.1.call-update) | async-done | bytes 835600 | tf_op jit(solution)/shard_map/reduce_scatter | solution.py:26
  486.4 1.3 multiply_convert_fusion.2
  487.6 0.8 pad_maximum_fusion.2
  488.4 0.0 all-gather.2.cloned.1.call-update
  488.5 0.0 copy-start.2
  488.5 140.3 %all-gather.2.cloned.1.call-done = bf16[1088,768]{1,0:T(8,128)(2,1)} async-done(((bf16[272,768]{1,0:T(8,128)(2,1)}), bf16[1088,768]{1,0:T(8,128)(2,1)}) %all-gather.2.cloned.1.call-update) | async-done | bytes 1671184 | tf_op jit(solution)/shard_map/all_gather | solution.py:39
  628.7 1.8 fusion.10
  630.6 0.0 copy-done.2
  630.6 3.2 fusion
  633.7 4.0 reshape.115
  637.7 13.9 %all-to-all-start.1 = ((bf16[32,34,896]{2,1,0:T(8,128)(2,1)}), bf16[32,34,896]{2,1,0:T(8,128)(2,1)}, u32[]{:S(2)}, u32[]{:S(2)}) async-start(bf16[32,34,896]{2,1,0:T(8,128)(2,1)} %reshape.115), calls=%async_computation.2 | async-start | bytes 4587520 | tf_op jit(solution)/shard_map/all_to_all | solution.py:135
  651.6 3.2 fusion.3
  654.8 2.6 fusion.2
  657.5 98.1 %all-to-all-done.1 = bf16[32,34,896]{2,1,0:T(8,128)(2,1)} async-done(((bf16[32,34,896]{2,1,0:T(8,128)(2,1)}), bf16[32,34,896]{2,1,0:T(8,128)(2,1)}, u32[]{:S(2)}, u32[]{:S(2)}) %all-to-all-start.1) | async-done | bytes 1949728 | tf_op jit(solution)/shard_map/all_to_all | solution.py:135
  755.5 3.1 convert_reduce_fusion
  758.6 1.4 reshape.116
  760.0 2.0 gather_fusion
  762.0 1.4 reshape.117
  763.5 0.6 reduce_sum.40
  764.1 3.8 collective-permute-start
  767.8 2.6 fusion.1
  770.5 2.2 collective-permute-done
  772.7 0.6 copy.16
  (7 shorter events, 0.1 us)
Async XLA Ops:
  7.2 214.3 %copy-start = (bf16[1,896,256]{2,1,0:T(8,128)(2,1)S(1)}, bf16[1,896,256]{2,1,0:T(8,128)(2,1)}, u32[]{:S(2)}) copy-start(bf16[1,896,256]{2,1,0:T(8,128)(2,1)} %param.11) | copy-start | bytes 1376260
  7.2 4.2 copy-start.4
  7.2 479.2 %reduce-scatter.2.cloned.1.call-start = ((), (), s32[]{:S(2)}) async-start(), calls=%async_computation.3 | async-start | bytes 4177920 | tf_op jit(solution)/shard_map/reduce_scatter | solution.py:26
  11.7 2.0 copy-start.3
  227.2 2.4 copy-start.1
  231.6 397.1 %all-gather.2.cloned.1.call-start = ((), (), s32[]{:S(2)}) async-start(), calls=%async_computation.4 | async-start | bytes 2088960 | tf_op jit(solution)/shard_map/all_gather | solution.py:39
  488.5 142.1 %copy-start.2 = (bf16[1,896,256]{2,1,0:T(8,128)(2,1)S(1)}, bf16[1,896,256]{2,1,0:T(8,128)(2,1)}, u32[]{:S(2)}) copy-start(bf16[1,896,256]{2,1,0:T(8,128)(2,1)} %param.12) | copy-start | bytes 1376260
  637.7 117.8 %all-to-all-start.1 = ((bf16[32,34,896]{2,1,0:T(8,128)(2,1)}), bf16[32,34,896]{2,1,0:T(8,128)(2,1)}, u32[]{:S(2)}, u32[]{:S(2)}) async-start(bf16[32,34,896]{2,1,0:T(8,128)(2,1)} %reshape.115), calls=%async_computation.2 | async-start | bytes 4587520 | tf_op jit(solution)/shard_map/all_to_all | solution.py:135
  764.1 8.6 %collective-permute-start = (bf16[1,64,896]{2,1,0:T(8,128)(2,1)S(1)}, bf16[1,64,896]{2,1,0:T(8,128)(2,1)S(1)}, u32[]{:S(2)}, u32[]{:S(2)}) collective-permute-start(bf16[1,64,896]{2,1,0:T(8,128)(2,1)S(1)} %bitcast.49), channel_id=1, source_target_pairs={{128,0},{256,128},{384,256},{512,384},{640,512},{768,640},{896,768... | collective-permute-start | bytes 344072 | tf_op jit(solution)/shard_map/ppermute | solution.py:45
Sparse Core Ops, SparseCore 0:
  231.8 254.5 reduce-scatter.1
  489.6 139.0 all-gather.1
where the time goes:
time: 781 us; the launch traced here: 780 us
  waiting for transfers between devices  495 us (63%)
  blocking collectives  197 us (25%)
  local copies, waits for them, and re-layouts  23.9 us (3%)
  matrix products  19.4 us (2%)
  starting transfers between devices  17.7 us (2%)
  between operations  14.3 us (2%)
  other arithmetic  13 us (2%)
    reduce_scatter x1, waiting for transfers between devices, in_one_piece_2(): lax.psum_scatter(both, axis, scatter_dimension=dim, tiled=True)  255 us
    all_to_all x1, blocking collectives, in_one_piece(): lax.all_to_all(both, axis, split_axis=split_dim, concat_axis=concat_dim,...  197 us
    all_gather x1, waiting for transfers between devices, side_by_side(): lax.all_gather(both, axis, axis=dim, tiled=True)  140 us
    all_to_all x1, waiting for transfers between devices, per_device(): lax.all_to_all(back_rows.reshape(n_groups, capacity, columns), 'expert',...  98.1 us
  transfers between devices with their start and end apart: 4, of which 4 were waited for; matrix products, arithmetic and copies ran while one was open for 1% of the time, Pallas kernels for 0%

commit v1 on v0

v1 whole, which is shorter than its diff:
```python
import jax
import jax.numpy as jnp
from jax import lax
from jax.experimental import pallas as pl
from jax.experimental.pallas import tpu as pltpu
from jax.sharding import PartitionSpec as P

MESH = pl.DeviceIdType.MESH
SHARES = 4
NY, NZ, NR = 4, 8, 4
EXPERTS = 8
TOK = 64
CAP = 34
D = 896
H = 256
ROWS = NZ * CAP
TOKS = NZ * TOK
HALF = TOK // 2
PARTS = ((0, 96), (96, 96), (192, 80))
VMEM_LIMIT = 60 * 1024 * 1024


def remote(src, dst, send_sem, recv_sem, **where):
    return pltpu.make_async_remote_copy(
        src_ref=src, dst_ref=dst, send_sem=send_sem, recv_sem=recv_sem,
        device_id=where, device_id_type=MESH,
    )


def rows_of(ref, start, size):
    return ref.at[pl.ds(pl.multiple_of(start, 16), size), :]


def grid_place():
    me = lax.axis_index("expert")
    y, z = me // NZ, me % NZ
    return me, y, z, (y + 1) % NY * NZ + z, (y + NY - 1) % NY * NZ + z


def greet(me, z, up, down):
    barrier = pltpu.get_barrier_semaphore()
    for peer in (up, down):
        pl.semaphore_signal(barrier, inc=1, device_id={"expert": peer}, device_id_type=MESH)

    @pl.when(z > 0)
    def _():
        pl.semaphore_signal(barrier, inc=1, device_id={"expert": me - 1}, device_id_type=MESH)

    @pl.when(z < NZ - 1)
    def _():
        pl.semaphore_signal(barrier, inc=1, device_id={"expert": me + 1}, device_id_type=MESH)

    pl.semaphore_wait(barrier, 4 - (NZ - z) // NZ - (z + 1) // NZ)


def gather_kernel(b_ref, m_ref, ball, mall, own_sem,
                  zb_send, zb_recv, zm_send, zm_recv,
                  yb_send, yb_recv, ym_send, ym_recv,
                  fb_send, fb_recv, fm_send, fm_recv):
    me, y, z, up, down = grid_place()
    greet(me, z, up, down)
    own_b = pltpu.make_async_copy(b_ref, rows_of(ball, me * TOK, TOK), own_sem.at[0])
    own_m = pltpu.make_async_copy(m_ref, mall.at[me], own_sem.at[1])
    own_b.start()
    own_m.start()
    own_b.wait()
    own_m.wait()
    sides = ((me + 1, z < NZ - 1), (me - 1, z > 0))
    peers = (up, down)

    def z_copies(side, t, zz):
        block = y * NZ + zz
        to = sides[side][0]
        b = rows_of(ball, block * TOK, TOK)
        return (
            remote(b, b, zb_send.at[side, t], zb_recv.at[side, t], expert=to),
            remote(mall.at[block], mall.at[block], zm_send.at[side, t], zm_recv.at[side, t], expert=to),
        )

    def y_copies(way, col, zz):
        block = col * NZ + zz
        b = rows_of(ball, block * TOK, TOK)
        return (
            remote(b, b, yb_send.at[way, zz], yb_recv.at[way, zz], expert=peers[way]),
            remote(mall.at[block], mall.at[block], ym_send.at[way, zz], ym_recv.at[way, zz], expert=peers[way]),
        )

    def far_copy(way, col, zz):
        b = rows_of(ball, (col * NZ + zz) * TOK + way * HALF, HALF)
        return remote(b, b, fb_send.at[way, zz], fb_recv.at[way, zz], expert=peers[way])

    def far_meta(col, zz):
        block = col * NZ + zz
        return remote(mall.at[block], mall.at[block], fm_send.at[zz], fm_recv.at[zz], expert=up)

    came_up, came_down, far = (y + NY - 1) % NY, (y + 1) % NY, (y + 2) % NY

    def step(t, carry):
        for side in (0, 1):
            zz = z + t if side else z - t
            inside = (zz >= 0) & (zz < NZ)

            @pl.when(inside & (t > 0))
            def _():
                for c in z_copies(side, t - 1, zz):
                    c.wait_recv()

            @pl.when(inside & sides[side][1])
            def _():
                for c in z_copies(side, t, zz):
                    c.start()

            @pl.when(inside & ((t > 0) if side else (t >= 0)))
            def _():
                for way in (0, 1):
                    for c in y_copies(way, y, zz):
                        c.start()

        for side in (0, 1):
            zz = z + (t - 1) if side else z - (t - 1)
            inside = (zz >= 0) & (zz < NZ) & ((t > 1) if side else (t > 0))

            @pl.when(inside)
            def _():
                for c in y_copies(0, came_up, zz):
                    c.wait_recv()
                far_copy(0, came_up, zz).start()
                far_meta(came_up, zz).start()
                for c in y_copies(1, came_down, zz):
                    c.wait_recv()
                far_copy(1, came_down, zz).start()

        return carry

    lax.fori_loop(0, NZ + 1, step, 0)

    def finish(zz, carry):
        for way in (0, 1):
            far_copy(way, far, zz).wait_recv()
            far_copy(way, (came_up, came_down)[way], zz).wait_send()
            for c in y_copies(way, y, zz):
                c.wait_send()
        far_meta(far, zz).wait_recv()
        far_meta(came_up, zz).wait_send()
        for side in (0, 1):
            src = z + zz if side else z - zz

            @pl.when((src >= 0) & (src < NZ) & sides[side][1])
            def _():
                for c in z_copies(side, zz, src):
                    c.wait_send()

        return carry

    lax.fori_loop(0, NZ, finish, 0)


def all_tokens(block, meta):
    dma = pltpu.SemaphoreType.DMA
    return pl.pallas_call(
        gather_kernel,
        out_shape=(
            jax.ShapeDtypeStruct((NY * TOKS, 2 * D), jnp.bfloat16),
            jax.ShapeDtypeStruct((NY * NZ, 16, 128), jnp.float32),
        ),
        in_specs=[pl.BlockSpec(memory_space=pltpu.VMEM)] * 2,
        out_specs=(pl.BlockSpec(memory_space=pltpu.VMEM),) * 2,
        scratch_shapes=[dma((2,))] + [dma((2, NZ))] * 10 + [dma((NZ,))] * 2,
        compiler_params=pltpu.CompilerParams(
            collective_id=0, has_side_effects=True, vmem_limit_bytes=24 * 1024 * 1024
        ),
    )(block, meta)


def over_rows(left, right):
    return lax.dot_general(
        left, right, (((0,), (0,)), ((), ())), preferred_element_type=jnp.float32
    )


def over_cols(left, right):
    return lax.dot_general(
        left, right, (((1,), (1,)), ((), ())), preferred_element_type=jnp.float32
    )


def expert_kernel(ball, mall, wg, wu, wd, t_ref, gg, gu, gd,
                  pick, xs, gs, part, snd, rcv, act, wcat, back, gacc,
                  rs_send, rs_recv, ag_send, ag_recv):
    r = lax.axis_index("replica")
    e = lax.axis_index("expert") // SHARES
    nxt, prv = (r + 1) % NR, (r + NR - 1) % NR
    peers = (nxt, prv)
    barrier = pltpu.get_barrier_semaphore()
    for peer in peers:
        pl.semaphore_signal(barrier, inc=1, device_id={"replica": peer}, device_id_type=MESH)

    for d in (0, 1):
        wcat[d, :, 0:128] = wg[:, 128 * d:128 * d + 128]
        wcat[d, :, 128:256] = wu[:, 128 * d:128 * d + 128]

    lane = lax.broadcasted_iota(jnp.int32, (1, 128), 1)
    first = lane < TOK
    row = lax.broadcasted_iota(jnp.int32, (ROWS, 128), 0).astype(jnp.float32)
    which = lax.broadcasted_iota(jnp.int32, (NZ, EXPERTS, 128), 1)

    pl.semaphore_wait(barrier, 2)

    def rs_copy(d, s, k):
        at, size = PARTS[k]
        return remote(snd.at[d, s, at:at + size, :], rcv.at[d, s, at:at + size, :],
                      rs_send.at[d, s, k], rs_recv.at[d, s, k], replica=peers[d])

    def stage(d, s, k, c):
        at, size = PARTS[k]
        rows = pl.ds(pl.multiple_of(c * ROWS + at, 16), size)
        for kind in range(3):
            mine = part[rows, 256 * kind + 128 * d:256 * kind + 128 * d + 128]
            if s:
                mine = mine + rcv[d, s - 1, at:at + size, 128 * kind:128 * kind + 128].astype(jnp.float32)
            snd[d, s, at:at + size, 128 * kind:128 * kind + 128] = mine.astype(jnp.bfloat16)
        rs_copy(d, s, k).start()

    def chunk(q, carry):
        c = (r + 3 - 2 * q + 3 * (q // 2)) % NR
        rows = pl.ds(pl.multiple_of(c * ROWS, 16), ROWS)
        toks = pl.ds(pl.multiple_of(c * TOKS, 16), TOKS)
        meta = mall[pl.ds(c * NZ, NZ)]
        slots = jnp.sum(jnp.where(which == e, meta[:, 0:8, :], 0.0), axis=1)
        scale = jnp.sum(jnp.where(which == e, meta[:, 8:16, :], 0.0), axis=1)
        total = jnp.zeros((ROWS, 128), jnp.float32)
        for p in range(NZ // 2):
            slot = jnp.where(first, slots[2 * p:2 * p + 1], slots[2 * p + 1:2 * p + 2])
            w = jnp.where(first, scale[2 * p:2 * p + 1], scale[2 * p + 1:2 * p + 2])
            base = jnp.where(first, float(CAP * 2 * p), float(CAP * (2 * p + 1)))
            goal = jnp.where(slot >= 0.0, slot + base, -1.0)
            hit = row == goal
            total = total + jnp.where(hit, w, 0.0)
            pick[rows, 128 * p:128 * p + 128] = jnp.where(hit, 1.0, 0.0).astype(jnp.bfloat16)
        weight = jnp.sum(total, axis=1, keepdims=True)
        sel = pick[rows, :]
        x = jnp.dot(sel, ball[toks, 0:D], preferred_element_type=jnp.float32).astype(jnp.bfloat16)
        xs[rows, :] = x
        g = jnp.dot(sel, ball[toks, D:2 * D], preferred_element_type=jnp.float32)
        g = (g * weight).astype(jnp.bfloat16)
        gs[rows, :] = g
        part[rows, 0:256] = jnp.dot(x, wg[...], preferred_element_type=jnp.float32)
        part[rows, 256:512] = jnp.dot(x, wu[...], preferred_element_type=jnp.float32)
        part[rows, 512:768] = jnp.dot(g, wd[...], preferred_element_type=jnp.float32)
        for d in (0, 1):
            @pl.when(q == d)
            def _():
                for k in range(len(PARTS)):
                    stage(d, 0, k, c)

        return carry

    lax.fori_loop(0, NR, chunk, 0)

    for s in (1, 2):
        for k in range(len(PARTS)):
            for d in (0, 1):
                rs_copy(d, s - 1, k).wait_recv()
                stage(d, s, k, (r + NR - 1 - s) % NR if d == 0 else (r + 1 + s) % NR)

    def ag_copy(d, s, k, c):
        at, size = PARTS[k]
        there = act.at[d, pl.ds(pl.multiple_of(c * ROWS + at, 16), size), :]
        return remote(there, there, ag_send.at[d, s, k], ag_recv.at[d, s, k], replica=peers[d])

    for k, (at, size) in enumerate(PARTS):
        for d in (0, 1):
            rs_copy(d, 2, k).wait_recv()
            rows = pl.ds(pl.multiple_of(r * ROWS + at, 16), size)
            full = [
                part[rows, 256 * kind + 128 * d:256 * kind + 128 * d + 128]
                + rcv[d, 2, at:at + size, 128 * kind:128 * kind + 128].astype(jnp.float32)
                for kind in range(3)
            ]
            gate, up, dh = full
            sg = jax.nn.sigmoid(gate)
            a = gate * sg
            act[d, rows, 0:128] = (a * up).astype(jnp.bfloat16)
            act[d, rows, 128:256] = (dh * up * (sg * (1.0 + gate * (1.0 - sg)))).astype(jnp.bfloat16)
            act[d, rows, 256:384] = (dh * a).astype(jnp.bfloat16)
            ag_copy(d, 0, k, r).start()

    def spread(c):
        rows = pl.ds(pl.multiple_of(c * ROWS, 16), ROWS)
        toks = pl.ds(pl.multiple_of(c * TOKS, 16), TOKS)
        t_ref[toks, :] = over_rows(pick[rows, :], back[rows, :].astype(jnp.bfloat16)).astype(jnp.bfloat16)

    def arrive(k, carry):
        for d in (0, 1):
            c = (r + NR - k) % NR if d == 0 else (r + k) % NR

            @pl.when(k > 0)
            def _():
                for piece in range(len(PARTS)):
                    ag_copy(d, k - 1, piece, c).wait_recv()

                    @pl.when(k < NR - 1)
                    def _():
                        ag_copy(d, k, piece, c).start()

        for d in (0, 1):
            c = (r + NR - k) % NR if d == 0 else (r + k) % NR
            rows = pl.ds(pl.multiple_of(c * ROWS, 16), ROWS)
            both = act[d, rows, 128:384]
            more = over_cols(both, wcat[d])
            fresh = k < 3 if d == 0 else k == 1

            @pl.when(fresh)
            def _():
                back[rows, :] = more

            @pl.when(jnp.logical_not(fresh))
            def _():
                back[rows, :] = back[rows, :] + more

            up_down = over_rows(xs[rows, :], both)
            hid = over_rows(gs[rows, :], act[d, rows, 0:128])

            @pl.when(k == 0)
            def _():
                gacc[d, :, 128:384] = up_down
                gacc[d, :, 0:128] = hid

            @pl.when(k > 0)
            def _():
                gacc[d, :, 128:384] = gacc[d, :, 128:384] + up_down
                gacc[d, :, 0:128] = gacc[d, :, 0:128] + hid

        @pl.when(k % 2 == 0)
        def _():
            spread((r + k) % NR)

        @pl.when(k == 3)
        def _():
            spread((r + 1) % NR)
            spread((r + 3) % NR)

        return carry

    lax.fori_loop(0, NR, arrive, 0)

    for d in (0, 1):
        cols = slice(128 * d, 128 * d + 128)
        gd[:, cols] = gacc[d, :, 0:128].astype(jnp.bfloat16)
        gg[:, cols] = gacc[d, :, 128:256].astype(jnp.bfloat16)
        gu[:, cols] = gacc[d, :, 256:384].astype(jnp.bfloat16)
        for s in range(3):
            for k in range(len(PARTS)):
                rs_copy(d, s, k).wait_send()
                ag_copy(d, s, k, (r + NR - s) % NR if d == 0 else (r + s) % NR).wait_send()


def experts(tokens, meta, wg, wu, wd):
    dma = pltpu.SemaphoreType.DMA
    vm = pltpu.VMEM
    n = len(PARTS)
    return pl.pallas_call(
        expert_kernel,
        out_shape=(jax.ShapeDtypeStruct((NY * TOKS, D), jnp.bfloat16),)
        + (jax.ShapeDtypeStruct((D, H), jnp.bfloat16),) * 3,
        in_specs=[pl.BlockSpec(memory_space=pltpu.VMEM)] * 5,
        out_specs=(pl.BlockSpec(memory_space=pltpu.VMEM),) * 4,
        scratch_shapes=[
            vm((NR * ROWS, TOKS), jnp.bfloat16),
            vm((NR * ROWS, D), jnp.bfloat16),
            vm((NR * ROWS, D), jnp.bfloat16),
            vm((NR * ROWS, 3 * H), jnp.float32),
            vm((2, 3, ROWS, 384), jnp.bfloat16),
            vm((2, 3, ROWS, 384), jnp.bfloat16),
            vm((2, NR * ROWS, 384), jnp.bfloat16),
            vm((2, D, 256), jnp.bfloat16),
            vm((NR * ROWS, D), jnp.float32),
            vm((2, D, 384), jnp.float32),
            dma((2, 3, n)), dma((2, 3, n)), dma((2, 3, n)), dma((2, 3, n)),
        ],
        compiler_params=pltpu.CompilerParams(
            collective_id=1, has_side_effects=True, vmem_limit_bytes=VMEM_LIMIT
        ),
    )(tokens, meta, wg, wu, wd)


def return_kernel(t_ref, o_ref, ysnd, yrcv, col, zsnd, zrcv,
                  y_send, y_recv, z_send, z_recv):
    me, y, z, up, down = grid_place()
    greet(me, z, up, down)
    peers = (up, down)
    sides = ((me + 1, z < NZ - 1, z > 0), (me - 1, z > 0, z < NZ - 1))

    def block(c, zz, h):
        return pl.ds(pl.multiple_of(c * TOKS + zz * TOK + h * HALF, 16), HALF)

    def first(h, zz):
        c = (y + NY - 1) % NY if h == 0 else (y + 1) % NY
        return remote(t_ref.at[block(c, zz, h), :], yrcv.at[h, 0, zz],
                      y_send.at[h, 0, zz], y_recv.at[h, 0, zz], expert=peers[h])

    def later(h, s, zz):
        return remote(ysnd.at[h, s - 1, zz], yrcv.at[h, s, zz],
                      y_send.at[h, s, zz], y_recv.at[h, s, zz], expert=peers[h])

    def start(zz, carry):
        for h in (0, 1):
            first(h, zz).start()
        return carry

    lax.fori_loop(0, NZ, start, 0)
    for s in (1, 2, 3):
        def turn(zz, carry):
            for h in (0, 1):
                c = (y + 2 * NY - 1 - s) % NY if h == 0 else (y + 1 + s) % NY
                (first(h, zz) if s == 1 else later(h, s - 1, zz)).wait_recv()
                now = (t_ref[block(c, zz, h), :].astype(jnp.float32)
                       + yrcv[h, s - 1, zz].astype(jnp.float32))
                if s < 3:
                    ysnd[h, s - 1, zz] = now.astype(jnp.bfloat16)
                    later(h, s, zz).start()
                else:
                    col[h, zz] = now
            return carry

        lax.fori_loop(0, NZ, turn, 0)

    def z_copy(side, h, zz):
        return remote(zsnd.at[side, h, zz], zrcv.at[side, h, zz],
                      z_send.at[side, h, zz], z_recv.at[side, h, zz], expert=sides[side][0])

    def slot(tau, carry):
        for h in (0, 1):
            for side in (0, 1):
                zz = tau - (NZ - 1) + z if side else NZ - 1 - tau + z
                live = (zz >= 0) if side else (zz < NZ)

                @pl.when(live & sides[side][1] & sides[side][2])
                def _():
                    z_copy(side, h, zz).wait_recv()
                    zsnd[side, h, zz] = col[h, zz] + zrcv[side, h, zz]
                    z_copy(side, h, zz).start()

                @pl.when(live & sides[side][1] & jnp.logical_not(sides[side][2]))
                def _():
                    zsnd[side, h, zz] = col[h, zz]
                    z_copy(side, h, zz).start()

        return carry

    lax.fori_loop(0, NZ - 1, slot, 0)

    for h in (0, 1):
        for side in (0, 1):
            @pl.when(sides[side][2])
            def _():
                z_copy(side, h, z).wait_recv()
                col[h, z] = col[h, z] + zrcv[side, h, z]

        o_ref[h * HALF:h * HALF + HALF, :] = col[h, z].astype(jnp.bfloat16)

    def finish(zz, carry):
        for h in (0, 1):
            first(h, zz).wait_send()
            for s in (1, 2):
                later(h, s, zz).wait_send()

            @pl.when(zz > z)
            def _():
                z_copy(0, h, zz).wait_send()

            @pl.when(zz < z)
            def _():
                z_copy(1, h, zz).wait_send()

        return carry

    lax.fori_loop(0, NZ, finish, 0)


def home(table):
    dma = pltpu.SemaphoreType.DMA
    vm = pltpu.VMEM
    return pl.pallas_call(
        return_kernel,
        out_shape=jax.ShapeDtypeStruct((TOK, D), jnp.bfloat16),
        in_specs=[pl.BlockSpec(memory_space=pltpu.VMEM)],
        out_specs=pl.BlockSpec(memory_space=pltpu.VMEM),
        scratch_shapes=[
            vm((2, 2, NZ, HALF, D), jnp.bfloat16),
            vm((2, 3, NZ, HALF, D), jnp.bfloat16),
            vm((2, NZ, HALF, D), jnp.float32),
            vm((2, 2, NZ, HALF, D), jnp.float32),
            vm((2, 2, NZ, HALF, D), jnp.float32),
            dma((2, 3, NZ)), dma((2, 3, NZ)), dma((2, 2, NZ)), dma((2, 2, NZ)),
        ],
        compiler_params=pltpu.CompilerParams(
            collective_id=2, has_side_effects=True, vmem_limit_bytes=32 * 1024 * 1024
        ),
    )(table)


def shifted(value, axis, steps):
    count = lax.axis_size(axis)
    first, last = (max(0, -steps), min(count, count - steps))
    return lax.ppermute(value, axis, [(source, source + steps) for source in range(first, last)])


def table_of(routes, weights):
    chosen = routes.T[None] == jnp.arange(EXPERTS, dtype=jnp.int32)[:, None, None]
    named = jnp.sum(chosen.astype(jnp.float32), axis=1)
    weight = jnp.sum(jnp.where(chosen, weights.T[None], 0.0), axis=1)
    earlier = (jnp.arange(TOK)[:, None] < jnp.arange(TOK)[None, :]).astype(jnp.bfloat16)
    slot = jnp.dot(named.astype(jnp.bfloat16), earlier, preferred_element_type=jnp.float32)
    slot = jnp.where(named > 0.0, slot, -1.0)
    both = jnp.concatenate([slot, weight], axis=0)
    return jnp.concatenate([both, both], axis=1)


def per_device(token_grads, routing, gate_weights, layer_inputs, w_gate, w_up, w_down):
    block = jnp.concatenate([layer_inputs[0], token_grads[0]], axis=1)
    meta = table_of(routing[0], gate_weights[0])
    tokens, metas = all_tokens(block, meta)
    table, grad_gate, grad_up, grad_down = experts(tokens, metas, w_gate[0], w_up[0], w_down[0])
    upstream = shifted(home(table)[None], "section", -1)
    return (upstream, grad_gate[None], grad_up[None], grad_down[None])


def solution(mesh):
    placed = (
        P("section", "expert", "replica"),
        P("section", "expert", None),
        P("section", "expert", None),
        P("section", "expert", "replica"),
        P("section", "replica", "expert"),
        P("section", "replica", "expert"),
        P("section", "replica", "expert"),
    )
    return jax.shard_map(
        per_device,
        mesh=mesh,
        in_specs=placed,
        out_specs=(
            P("section", "expert", "replica"),
            P("section", "replica", "expert"),
            P("section", "replica", "expert"),
            P("section", "replica", "expert"),
        ),
        check_vma=False,
    )
```

time: 781 us -> 427 us (0.55)
  the two profiles are of different devices: /device:TPU:43 before, /device:TPU:11 now
where the time goes in v1:
time: 427 us
  Pallas kernels  403 us (94%)
  local copies, waits for them, and re-layouts  11.8 us (3%)
  starting transfers between devices  5.73 us (1%)
    pallas_call x1, Pallas kernels, experts(): pl.pallas_call(expert_kernel, out_shape=(jax.ShapeDtypeStruct((NY * TOKS,...  231 us
    pallas_call x1, Pallas kernels, home(): pl.pallas_call(return_kernel, out_shape=jax.ShapeDtypeStruct((TOK, D), jn...  103 us
    pallas_call x1, Pallas kernels, all_tokens(): pl.pallas_call(gather_kernel, out_shape=(jax.ShapeDtypeStruct((NY * TOKS,...  68.9 us
    unnamed x10, local copies, waits for them, and re-layouts  11.8 us
  transfers between devices with their start and end apart: 1, of which 1 were waited for; matrix products, arithmetic and copies ran while one was open for 0% of the time, Pallas kernels for 0%

profile of v1, /device:TPU:11, one launch (start us, length us, event | category | flops | bytes accessed | tf_op | source)
XLA Modules:
  0.0 426.8 jit_solution(12135288035208009003)
XLA Ops:
  0.6 0.7 convert_reduce_fusion
  1.3 0.1 convolution_select_fusion
  1.5 0.1 maximum_maximum_fusion.m_ref
  1.5 1.0 pad_maximum_fusion.b_ref
  2.5 68.9 %shard_map.102 = (bf16[2048,1792]{1,0:T(8,128)(2,1)S(1)}, f32[32,16,128]{2,1,0:T(8,128)S(1)}) custom-call(bf16[64,1792]{1,0:T(8,128)(2,1)S(1)} %pad_maximum_fusion.b_ref, f32[16,128]{1,0:T(8,128)S(1)} %maximum_maximum_fusion.m_ref), custom_call_target="tpu_custom_call" | custom-call | tf_op jit(solution)/shard_map/pallas_call | solution.py:160
  71.5 0.0 copy-start
  71.5 3.0 copy-done
  74.4 0.0 copy-start.2
  74.4 0.7 copy-done.2
  75.1 230.7 %shard_map.103 = (bf16[2048,896]{1,0:T(8,128)(2,1)}, bf16[896,256]{1,0:T(8,128)(2,1)}, bf16[896,256]{1,0:T(8,128)(2,1)}, bf16[896,256]{1,0:T(8,128)(2,1)}) custom-call(bf16[2048,1792]{1,0:T(8,128)(2,1)} %copy-done, f32[32,16,128]{2,1,0:T(8,128)} %copy-done.2, bf16[896,256]{1,0:T(8,128)(2,1)} %bitcast.19, bf16[896,256]{1,0:T(8,128)(2,1)} %bitcast.20, ...), custom_call_target="tpu_custom_call" | custom-call | tf_op jit(solution)/shard_map/pallas_call | solution.py:362
  305.8 0.0 copy-start.1
  305.8 2.0 copy-done.1
  307.9 103.5 %shard_map.104 = bf16[64,896]{1,0:T(8,128)(2,1)S(1)} custom-call(bf16[2048,896]{1,0:T(8,128)(2,1)S(1)} %copy-done.1), custom_call_target="tpu_custom_call" | custom-call | tf_op jit(solution)/shard_map/pallas_call | solution.py:484
  411.3 5.7 %collective-permute-start = (bf16[1,64,896]{2,1,0:T(8,128)(2,1)S(1)}, bf16[1,64,896]{2,1,0:T(8,128)(2,1)S(1)}, u32[]{:S(2)}, u32[]{:S(2)}) collective-permute-start(bf16[1,64,896]{2,1,0:T(8,128)(2,1)S(1)} %bitcast.15), channel_id=1, source_target_pairs={{128,0},{256,128},{384,256},{512,384},{640,512},{768,640},{896,768... | collective-permute-start | bytes 344072 | tf_op jit(solution)/shard_map/ppermute | solution.py:506
  417.1 3.7 collective-permute-done
  420.7 0.6 copy.15
  421.4 1.8 copy.16
  423.2 1.8 copy.17
  425.0 1.8 copy.18
Async XLA Ops:
  71.5 3.0 copy-start
  74.4 0.7 copy-start.2
  305.8 2.0 copy-start.1
  411.3 9.4 %collective-permute-start = (bf16[1,64,896]{2,1,0:T(8,128)(2,1)S(1)}, bf16[1,64,896]{2,1,0:T(8,128)(2,1)S(1)}, u32[]{:S(2)}, u32[]{:S(2)}) collective-permute-start(bf16[1,64,896]{2,1,0:T(8,128)(2,1)S(1)} %bitcast.15), channel_id=1, source_target_pairs={{128,0},{256,128},{384,256},{512,384},{640,512},{768,640},{896,768... | collective-permute-start | bytes 344072 | tf_op jit(solution)/shard_map/ppermute | solution.py:506

commit v2 on v1

v2 whole, which is shorter than its diff:
```python
import jax
import jax.numpy as jnp
from jax import lax
from jax.experimental import pallas as pl
from jax.experimental.pallas import tpu as pltpu
from jax.sharding import PartitionSpec as P

MESH = pl.DeviceIdType.MESH
SHARES = 4
NY, NZ, NR = 4, 8, 4
EXPERTS = 8
TOK = 64
CAP = 34
D = 896
H = 256
ROWS = NZ * CAP
TOKS = NZ * TOK
HALF = TOK // 2
PIECE, REST = 64, 16
COLUMN = (0, 1, 3, 2)
VMEM_LIMIT = 60 * 1024 * 1024


def remote(src, dst, send_sem, recv_sem, **where):
    return pltpu.make_async_remote_copy(
        src_ref=src, dst_ref=dst, send_sem=send_sem, recv_sem=recv_sem,
        device_id=where, device_id_type=MESH,
    )


def rows_of(ref, start, size):
    return ref.at[pl.ds(pl.multiple_of(start, 16), size), :]


def grid_place():
    me = lax.axis_index("expert")
    y, z = me // NZ, me % NZ
    return me, y, z, (y + 1) % NY * NZ + z, (y + NY - 1) % NY * NZ + z


def over_rows(left, right):
    return lax.dot_general(
        left, right, (((0,), (0,)), ((), ())), preferred_element_type=jnp.float32
    )


def over_cols(left, right):
    return lax.dot_general(
        left, right, (((1,), (1,)), ((), ())), preferred_element_type=jnp.float32
    )


def kernel(b_ref, m_ref, wg, wu, wd, o_ref, gg, gu, gd,
           ball, mall, pick, picks, xs, gs, part, snd, rcv, snd_rest, rcv_rest, act, wcat, gacc,
           bsnd, brcv, total, zsnd, zrcv, own_sem,
           zb_send, zb_recv, zm_send, zm_recv, yb_send, yb_recv, ym_send, ym_recv,
           fb_send, fb_recv, fm_send, fm_recv, rs_send, rs_recv, ag_send, ag_recv,
           b_send, b_recv, z_send, z_recv):
    me, y, z, up, down = grid_place()
    r = lax.axis_index("replica")
    peers = (up, down)
    rings = ((r + 1) % NR, (r + NR - 1) % NR)
    far_off = (y + 2) % NY * NZ + z
    sides = ((me + 1, z < NZ - 1, z > 0), (me - 1, z > 0, z < NZ - 1))

    barrier = pltpu.get_barrier_semaphore()
    for peer in (up, down, far_off):
        pl.semaphore_signal(barrier, inc=1, device_id={"expert": peer}, device_id_type=MESH)
    for peer in rings:
        pl.semaphore_signal(barrier, inc=1, device_id={"replica": peer}, device_id_type=MESH)
    for side in (0, 1):
        @pl.when(sides[side][1])
        def _():
            pl.semaphore_signal(barrier, inc=1, device_id={"expert": sides[side][0]}, device_id_type=MESH)

    pl.semaphore_wait(barrier, 7 - (NZ - z) // NZ - (z + 1) // NZ)

    own_b = pltpu.make_async_copy(b_ref, rows_of(ball, me * TOK, TOK), own_sem.at[0])
    own_m = pltpu.make_async_copy(m_ref, mall.at[me], own_sem.at[1])
    own_b.start()
    own_m.start()
    own_b.wait()
    own_m.wait()

    def z_copies(side, t, zz):
        at = y * NZ + zz
        to = sides[side][0]
        b = rows_of(ball, at * TOK, TOK)
        return (
            remote(b, b, zb_send.at[side, t], zb_recv.at[side, t], expert=to),
            remote(mall.at[at], mall.at[at], zm_send.at[side, t], zm_recv.at[side, t], expert=to),
        )

    def y_copies(way, col, zz):
        at = col * NZ + zz
        b = rows_of(ball, at * TOK, TOK)
        return (
            remote(b, b, yb_send.at[way, zz], yb_recv.at[way, zz], expert=peers[way]),
            remote(mall.at[at], mall.at[at], ym_send.at[way, zz], ym_recv.at[way, zz], expert=peers[way]),
        )

    def far_copy(way, col, zz):
        b = rows_of(ball, (col * NZ + zz) * TOK + way * HALF, HALF)
        return remote(b, b, fb_send.at[way, zz], fb_recv.at[way, zz], expert=peers[way])

    def far_meta(col, zz):
        at = col * NZ + zz
        return remote(mall.at[at], mall.at[at], fm_send.at[zz], fm_recv.at[zz], expert=up)

    came_up, came_down, far = (y + NY - 1) % NY, (y + 1) % NY, (y + 2) % NY

    def along(t, carry):
        for side in (0, 1):
            zz = z + t if side else z - t
            inside = (zz >= 0) & (zz < NZ)

            @pl.when(inside & (t > 0))
            def _():
                for c in z_copies(side, t - 1, zz):
                    c.wait_recv()

            @pl.when(inside & sides[side][1])
            def _():
                for c in z_copies(side, t, zz):
                    c.start()

            @pl.when(inside & ((t > 0) if side else (t >= 0)))
            def _():
                for way in (0, 1):
                    for c in y_copies(way, y, zz):
                        c.start()

        return carry

    lax.fori_loop(0, NZ, along, 0)

    def round_y(t, carry):
        for side in (0, 1):
            zz = z + t if side else z - t

            @pl.when((zz >= 0) & (zz < NZ) & ((t > 0) if side else (t >= 0)))
            def _():
                for c in y_copies(0, came_up, zz):
                    c.wait_recv()
                far_copy(0, came_up, zz).start()
                far_meta(came_up, zz).start()
                for c in y_copies(1, came_down, zz):
                    c.wait_recv()
                far_copy(1, came_down, zz).start()

        return carry

    def round_far(zz, carry):
        for way in (0, 1):
            far_copy(way, far, zz).wait_recv()
        far_meta(far, zz).wait_recv()
        return carry

    lane = lax.broadcasted_iota(jnp.int32, (1, 128), 1)
    first = lane < TOK
    row = lax.broadcasted_iota(jnp.int32, (ROWS, 128), 0).astype(jnp.float32)
    which = lax.broadcasted_iota(jnp.int32, (NZ, EXPERTS, 128), 1)

    def choose(to, at, c, e):
        meta = mall[pl.ds(c * NZ, NZ)]
        slots = jnp.sum(jnp.where(which == e, meta[:, 0:8, :], 0.0), axis=1)
        scale = jnp.sum(jnp.where(which == e, meta[:, 8:16, :], 0.0), axis=1)
        weight = jnp.zeros((ROWS, 128), jnp.float32)
        for p in range(NZ // 2):
            slot = jnp.where(first, slots[2 * p:2 * p + 1], slots[2 * p + 1:2 * p + 2])
            w = jnp.where(first, scale[2 * p:2 * p + 1], scale[2 * p + 1:2 * p + 2])
            base = jnp.where(first, float(CAP * 2 * p), float(CAP * (2 * p + 1)))
            hit = row == jnp.where(slot >= 0.0, slot + base, -1.0)
            weight = weight + jnp.where(hit, w, 0.0)
            to[pl.ds(pl.multiple_of(at, 16), ROWS), 128 * p:128 * p + 128] = jnp.where(hit, 1.0, 0.0).astype(jnp.bfloat16)
        return jnp.sum(weight, axis=1, keepdims=True)

    def column(g):
        return (y + COLUMN[g]) % NY

    def column_rows(g):
        return pl.ds(pl.multiple_of(column(g) * ROWS, 16), ROWS)

    def products(g):
        c = column(g)
        rows = column_rows(g)
        toks = pl.ds(pl.multiple_of(c * TOKS, 16), TOKS)
        weight = choose(pick, c * ROWS, c, me // SHARES)
        sel = pick[rows, :]
        x = jnp.dot(sel, ball[toks, 0:D], preferred_element_type=jnp.float32).astype(jnp.bfloat16)
        xs[rows, :] = x
        gr = jnp.dot(sel, ball[toks, D:2 * D], preferred_element_type=jnp.float32)
        gr = (gr * weight).astype(jnp.bfloat16)
        gs[rows, :] = gr
        part[rows, 0:256] = jnp.dot(x, wg[...], preferred_element_type=jnp.float32)
        part[rows, 256:512] = jnp.dot(x, wu[...], preferred_element_type=jnp.float32)
        part[rows, 512:768] = jnp.dot(gr, wd[...], preferred_element_type=jnp.float32)

    def piece(g, o):
        if g < NY:
            return pl.ds(pl.multiple_of(column(g) * ROWS + o * PIECE, 16), PIECE)
        return pl.ds(pl.multiple_of(o * ROWS + NR * PIECE, 16), REST)

    def out_of(g):
        return (snd.at[g], rcv.at[g]) if g < NY else (snd_rest, rcv_rest)

    def rs_copy(g, d, s):
        a, b = out_of(g)
        return remote(a.at[d, s], b.at[d, s], rs_send.at[g, d, s], rs_recv.at[g, d, s], replica=rings[d])

    def stage(g, s):
        for d in (0, 1):
            o = (r + NR - 1 - s) % NR if d == 0 else (r + 1 + s) % NR
            rows = piece(g, o)
            a, b = out_of(g)
            if s:
                rs_copy(g, d, s - 1).wait_recv()
            for kind in range(3):
                mine = part[rows, 256 * kind + 128 * d:256 * kind + 128 * d + 128]
                cols = slice(128 * kind, 128 * kind + 128)
                if s:
                    mine = mine + b[d, s - 1, :, cols].astype(jnp.float32)
                a[d, s, :, cols] = mine.astype(jnp.bfloat16)
            rs_copy(g, d, s).start()

    def ag_copy(g, d, s):
        there = act.at[d, piece(g, (r + NR - s) % NR if d == 0 else (r + s) % NR), :]
        return remote(there, there, ag_send.at[g, d, s], ag_recv.at[g, d, s], replica=rings[d])

    def arrived(g, d, s):
        there = act.at[d, piece(g, (r + NR - 1 - s) % NR if d == 0 else (r + 1 + s) % NR), :]
        return remote(there, there, ag_send.at[g, d, s], ag_recv.at[g, d, s], replica=rings[d])

    def final(g):
        for d in (0, 1):
            rs_copy(g, d, 2).wait_recv()
            rows = piece(g, r)
            b = out_of(g)[1]
            gate, upp, dh = [
                part[rows, 256 * kind + 128 * d:256 * kind + 128 * d + 128]
                + b[d, 2, :, 128 * kind:128 * kind + 128].astype(jnp.float32)
                for kind in range(3)
            ]
            sg = jax.nn.sigmoid(gate)
            a = gate * sg
            act[d, rows, 0:128] = (a * upp).astype(jnp.bfloat16)
            act[d, rows, 128:256] = (dh * upp * (sg * (1.0 + gate * (1.0 - sg)))).astype(jnp.bfloat16)
            act[d, rows, 256:384] = (dh * a).astype(jnp.bfloat16)
            ag_copy(g, d, 0).start()

    def onward(g, s):
        for d in (0, 1):
            arrived(g, d, s - 1).wait_recv()
            if s < NR - 1:
                ag_copy(g, d, s).start()

    def back_copy(g):
        to = (me, up, down, far_off)[g]
        return remote(bsnd.at[g], brcv.at[g], b_send.at[g], b_recv.at[g], expert=to)

    def backward(g):
        rows = column_rows(g)
        back = over_cols(act[0, rows, 128:384], wcat[0]) + over_cols(act[1, rows, 128:384], wcat[1])
        if g:
            bsnd[g] = back.astype(jnp.bfloat16)
            back_copy(g).start()
        else:
            brcv[0] = back.astype(jnp.bfloat16)

    def weights(g, fresh):
        rows = column_rows(g)
        for d in (0, 1):
            up_down = over_rows(xs[rows, :], act[d, rows, 128:384])
            hid = over_rows(gs[rows, :], act[d, rows, 0:128])
            if fresh:
                gacc[d, :, 128:384] = up_down
                gacc[d, :, 0:128] = hid
            else:
                gacc[d, :, 128:384] = gacc[d, :, 128:384] + up_down
                gacc[d, :, 0:128] = gacc[d, :, 0:128] + hid

    def collect(g, fresh):
        if g:
            back_copy(g).wait_recv()
        mine = over_rows(picks[g], brcv[g])
        total[...] = mine if fresh else total[...] + mine

    products(0)
    stage(0, 0)
    for d in (0, 1):
        wcat[d, :, 0:128] = wg[:, 128 * d:128 * d + 128]
        wcat[d, :, 128:256] = wu[:, 128 * d:128 * d + 128]
    lax.fori_loop(0, NZ, round_y, 0)
    stage(0, 1)
    products(1)
    stage(1, 0)
    products(2)
    stage(2, 0)
    stage(0, 2)
    lax.fori_loop(0, NZ, round_far, 0)
    products(3)
    stage(4, 0)
    stage(3, 0)
    for g in (1, 2, 4, 3):
        stage(g, 1)
    for g in range(NY):
        choose(picks.at[g], 0, y, (y + (0, 3, 1, 2)[g]) % NY * 2 + z // SHARES)
    for g in (1, 2, 4, 3):
        stage(g, 2)
    final(1)
    final(2)
    final(4)
    onward(1, 1)
    final(3)
    onward(2, 1)
    onward(4, 1)
    onward(1, 2)
    final(0)
    onward(3, 1)
    onward(2, 2)
    onward(4, 2)
    onward(4, 3)
    onward(1, 3)
    backward(1)
    onward(3, 2)
    onward(0, 1)
    weights(1, True)
    onward(2, 3)
    backward(2)
    onward(0, 2)
    weights(2, False)
    onward(3, 3)
    backward(3)
    weights(3, False)
    collect(1, True)
    collect(2, False)
    onward(0, 3)
    backward(0)
    collect(0, False)
    collect(3, False)

    def z_copy(side, h, zz):
        return remote(zsnd.at[side, h, zz], zrcv.at[side, h, zz],
                      z_send.at[side, h, zz], z_recv.at[side, h, zz], expert=sides[side][0])

    def of_group(h, zz):
        return total[pl.ds(pl.multiple_of(zz * TOK + h * HALF, 16), HALF), :]

    def slot(tau, carry):
        for h in (0, 1):
            for side in (0, 1):
                zz = tau - (NZ - 1) + z if side else NZ - 1 - tau + z
                live = (zz >= 0) if side else (zz < NZ)

                @pl.when(live & sides[side][1] & sides[side][2])
                def _():
                    z_copy(side, h, zz).wait_recv()
                    zsnd[side, h, zz] = (of_group(h, zz) + zrcv[side, h, zz].astype(jnp.float32)).astype(jnp.bfloat16)
                    z_copy(side, h, zz).start()

                @pl.when(live & sides[side][1] & jnp.logical_not(sides[side][2]))
                def _():
                    zsnd[side, h, zz] = of_group(h, zz).astype(jnp.bfloat16)
                    z_copy(side, h, zz).start()

        return carry

    lax.fori_loop(0, 1, slot, 0)
    weights(0, False)
    lax.fori_loop(1, NZ - 1, slot, 0)
    for h in (0, 1):
        at = pl.ds(pl.multiple_of(z * TOK + h * HALF, 16), HALF)
        for side in (0, 1):
            @pl.when(sides[side][2])
            def _():
                z_copy(side, h, z).wait_recv()
                total[at, :] = total[at, :] + zrcv[side, h, z].astype(jnp.float32)

        o_ref[h * HALF:h * HALF + HALF, :] = total[at, :].astype(jnp.bfloat16)

    for d in (0, 1):
        cols = slice(128 * d, 128 * d + 128)
        gd[:, cols] = gacc[d, :, 0:128].astype(jnp.bfloat16)
        gg[:, cols] = gacc[d, :, 128:256].astype(jnp.bfloat16)
        gu[:, cols] = gacc[d, :, 256:384].astype(jnp.bfloat16)

    def finish(zz, carry):
        for way in (0, 1):
            far_copy(way, (came_up, came_down)[way], zz).wait_send()
            for c in y_copies(way, y, zz):
                c.wait_send()
        far_meta(came_up, zz).wait_send()
        for side in (0, 1):
            src = z + zz if side else z - zz

            @pl.when((src >= 0) & (src < NZ) & sides[side][1])
            def _():
                for c in z_copies(side, zz, src):
                    c.wait_send()

        for h in (0, 1):
            @pl.when(zz > z)
            def _():
                z_copy(0, h, zz).wait_send()

            @pl.when(zz < z)
            def _():
                z_copy(1, h, zz).wait_send()

        return carry

    lax.fori_loop(0, NZ, finish, 0)
    for g in range(NY + 1):
        for d in (0, 1):
            for s in range(NR - 1):
                rs_copy(g, d, s).wait_send()
                ag_copy(g, d, s).wait_send()
    for g in (1, 2, 3):
        back_copy(g).wait_send()


def layer(tokens, meta, wg, wu, wd):
    dma = pltpu.SemaphoreType.DMA
    vm = pltpu.VMEM
    bf, f32 = jnp.bfloat16, jnp.float32
    rows = NR * ROWS
    return pl.pallas_call(
        kernel,
        out_shape=(jax.ShapeDtypeStruct((TOK, D), bf),) + (jax.ShapeDtypeStruct((D, H), bf),) * 3,
        in_specs=[pl.BlockSpec(memory_space=pltpu.VMEM)] * 5,
        out_specs=(pl.BlockSpec(memory_space=pltpu.VMEM),) * 4,
        scratch_shapes=[
            vm((NY * TOKS, 2 * D), bf), vm((NY * NZ, 16, 128), f32),
            vm((rows, TOKS), bf), vm((NY, ROWS, TOKS), bf),
            vm((rows, D), bf), vm((rows, D), bf), vm((rows, 3 * H), f32),
            vm((NY, 2, 3, PIECE, 384), bf), vm((NY, 2, 3, PIECE, 384), bf),
            vm((2, 3, REST, 384), bf), vm((2, 3, REST, 384), bf),
            vm((2, rows, 384), bf), vm((2, D, 256), bf), vm((2, D, 384), f32),
            vm((NY, ROWS, D), bf), vm((NY, ROWS, D), bf), vm((TOKS, D), f32),
            vm((2, 2, NZ, HALF, D), bf), vm((2, 2, NZ, HALF, D), bf),
            dma((2,)),
        ] + [dma((2, NZ))] * 10 + [dma((NZ,))] * 2 + [dma((NY + 1, 2, 3))] * 4
        + [dma((NY,))] * 2 + [dma((2, 2, NZ))] * 2,
        compiler_params=pltpu.CompilerParams(
            collective_id=0, has_side_effects=True, vmem_limit_bytes=VMEM_LIMIT
        ),
    )(tokens, meta, wg, wu, wd)


def shifted(value, axis, steps):
    count = lax.axis_size(axis)
    first, last = (max(0, -steps), min(count, count - steps))
    return lax.ppermute(value, axis, [(source, source + steps) for source in range(first, last)])


def table_of(routes, weights):
    chosen = routes.T[None] == jnp.arange(EXPERTS, dtype=jnp.int32)[:, None, None]
    named = jnp.sum(chosen.astype(jnp.float32), axis=1)
    weight = jnp.sum(jnp.where(chosen, weights.T[None], 0.0), axis=1)
    earlier = (jnp.arange(TOK)[:, None] < jnp.arange(TOK)[None, :]).astype(jnp.bfloat16)
    slot = jnp.dot(named.astype(jnp.bfloat16), earlier, preferred_element_type=jnp.float32)
    slot = jnp.where(named > 0.0, slot, -1.0)
    both = jnp.concatenate([slot, weight], axis=0)
    return jnp.concatenate([both, both], axis=1)


def per_device(token_grads, routing, gate_weights, layer_inputs, w_gate, w_up, w_down):
    block = jnp.concatenate([layer_inputs[0], token_grads[0]], axis=1)
    meta = table_of(routing[0], gate_weights[0])
    boundary, grad_gate, grad_up, grad_down = layer(block, meta, w_gate[0], w_up[0], w_down[0])
    upstream = shifted(boundary[None], "section", -1)
    return (upstream, grad_gate[None], grad_up[None], grad_down[None])


def solution(mesh):
    placed = (
        P("section", "expert", "replica"),
        P("section", "expert", None),
        P("section", "expert", None),
        P("section", "expert", "replica"),
        P("section", "replica", "expert"),
        P("section", "replica", "expert"),
        P("section", "replica", "expert"),
    )
    return jax.shard_map(
        per_device,
        mesh=mesh,
        in_specs=placed,
        out_specs=(
            P("section", "expert", "replica"),
            P("section", "replica", "expert"),
            P("section", "replica", "expert"),
            P("section", "replica", "expert"),
        ),
        check_vma=False,
    )
```

time: 427 us -> 364 us (0.85)
  the two profiles are of different devices: /device:TPU:11 before, /device:TPU:5 now
where the time goes in v2:
time: 364 us; the launch traced here: 363 us
  Pallas kernels  335 us (92%)
  starting transfers between devices  13.9 us (4%)
  waiting for transfers between devices  6.01 us (2%)
  local copies, waits for them, and re-layouts  5.14 us (1%)
    pallas_call x1, Pallas kernels, layer(): pl.pallas_call(kernel, out_shape=(jax.ShapeDtypeStruct((TOK, D), bf),) +...  335 us
    ppermute x1, starting transfers between devices, shifted(): lax.ppermute(value, axis, [(source, source + steps) for source in range(f...  13.9 us
  transfers between devices with their start and end apart: 1, of which 1 were waited for; matrix products, arithmetic and copies ran while one was open for 0% of the time, Pallas kernels for 0%

profile of v2, /device:TPU:5, one launch (start us, length us, event | category | flops | bytes accessed | tf_op | source)
XLA Modules:
  0.0 363.5 jit_solution(17798654349359019158)
XLA Ops:
  0.6 0.0 copy-start.2
  0.6 0.7 copy-done.2
  1.3 0.7 convert_reduce_fusion
  2.0 0.1 convolution_select_fusion
  2.1 0.7 maximum_maximum_fusion.m_ref
  2.8 1.7 pad_maximum_fusion.b_ref
  4.5 334.6 %shard_map.102 = (bf16[64,896]{1,0:T(8,128)(2,1)}, bf16[896,256]{1,0:T(8,128)(2,1)}, bf16[896,256]{1,0:T(8,128)(2,1)}, bf16[896,256]{1,0:T(8,128)(2,1)}) custom-call(bf16[64,1792]{1,0:T(8,128)(2,1)} %pad_maximum_fusion.b_ref, f32[16,128]{1,0:T(8,128)} %maximum_maximum_fusion.m_ref, bf16[896,256]{1,0:T(8,128)(2,1)} %bitcast.18, bf16[896,256]{1,0:T(8,128)(2,1)} %bitcast.19, ...), custom_call_target="tpu_custom_call" | custom-call | tf_op jit(solution)/shard_map/pallas_call | solution.py:427
  339.1 13.9 %collective-permute-start = (bf16[1,64,896]{2,1,0:T(8,128)(2,1)}, bf16[1,64,896]{2,1,0:T(8,128)(2,1)S(1)}, u32[]{:S(2)}, u32[]{:S(2)}) collective-permute-start(bf16[1,64,896]{2,1,0:T(8,128)(2,1)} %bitcast.25), channel_id=1, source_target_pairs={{128,0},{256,128},{384,256},{512,384},{640,512},{768,640},{896,768... | collective-permute-start | bytes 344072 | tf_op jit(solution)/shard_map/ppermute | solution.py:453
  353.0 6.0 %collective-permute-done = bf16[1,64,896]{2,1,0:T(8,128)(2,1)S(1)} collective-permute-done((bf16[1,64,896]{2,1,0:T(8,128)(2,1)}, bf16[1,64,896]{2,1,0:T(8,128)(2,1)S(1)}, u32[]{:S(2)}, u32[]{:S(2)}) %collective-permute-start) | collective-permute-done | bytes 114720 | tf_op jit(solution)/shard_map/ppermute | solution.py:453
  359.0 0.6 copy.15
  359.7 0.0 copy-start.1
  359.7 1.9 copy.16
  361.5 0.0 copy-done.1
  361.5 0.0 copy-start
  361.5 0.8 copy.17
  362.3 0.4 copy-done
  362.7 0.8 copy.18
Async XLA Ops:
  0.6 0.7 copy-start.2
  339.1 20.0 %collective-permute-start = (bf16[1,64,896]{2,1,0:T(8,128)(2,1)}, bf16[1,64,896]{2,1,0:T(8,128)(2,1)S(1)}, u32[]{:S(2)}, u32[]{:S(2)}) collective-permute-start(bf16[1,64,896]{2,1,0:T(8,128)(2,1)} %bitcast.25), channel_id=1, source_target_pairs={{128,0},{256,128},{384,256},{512,384},{640,512},{768,640},{896,768... | collective-permute-start | bytes 344072 | tf_op jit(solution)/shard_map/ppermute | solution.py:453
  359.7 1.9 copy-start.1
  361.5 1.2 copy-start

commit v3 on v2

--- a/solution.py
+++ b/solution.py
@@ -18,6 +18,8 @@
 HALF = TOK // 2
 PIECE, REST = 64, 16
 COLUMN = (0, 1, 3, 2)
+GROUPS = ((0, 0, 32), (1, 0, 64), (2, 0, 64), (3, 0, 64), None, (0, 32, 32))
+NS = 8
 VMEM_LIMIT = 60 * 1024 * 1024
 
 
@@ -52,12 +54,13 @@
 
 def kernel(b_ref, m_ref, wg, wu, wd, o_ref, gg, gu, gd,
            ball, mall, pick, picks, xs, gs, part, snd, rcv, snd_rest, rcv_rest, act, wcat, gacc,
-           bsnd, brcv, total, zsnd, zrcv, own_sem,
+           bsnd, brcv, total, zsnd, zrcv, edge, own_sem,
            zb_send, zb_recv, zm_send, zm_recv, yb_send, yb_recv, ym_send, ym_recv,
            fb_send, fb_recv, fm_send, fm_recv, rs_send, rs_recv, ag_send, ag_recv,
-           b_send, b_recv, z_send, z_recv):
+           b_send, b_recv, z_send, z_recv, s_send, s_recv):
     me, y, z, up, down = grid_place()
     r = lax.axis_index("replica")
+    sec = lax.axis_index("section")
     peers = (up, down)
     rings = ((r + 1) % NR, (r + NR - 1) % NR)
     far_off = (y + 2) % NY * NZ + z
@@ -73,7 +76,14 @@
         def _():
             pl.semaphore_signal(barrier, inc=1, device_id={"expert": sides[side][0]}, device_id_type=MESH)
 
-    pl.semaphore_wait(barrier, 7 - (NZ - z) // NZ - (z + 1) // NZ)
+    for near, there in ((sec - 1, sec > 0), (sec + 1, sec < NS - 1)):
+        @pl.when(there)
+        def _():
+            pl.semaphore_signal(barrier, inc=1, device_id={"section": near}, device_id_type=MESH)
+
+    pl.semaphore_wait(
+        barrier, 9 - (NZ - z) // NZ - (z + 1) // NZ - (NS - sec) // NS - (sec + 1) // NS
+    )
 
     own_b = pltpu.make_async_copy(b_ref, rows_of(ball, me * TOK, TOK), own_sem.at[0])
     own_m = pltpu.make_async_copy(m_ref, mall.at[me], own_sem.at[1])
@@ -82,22 +92,24 @@
     own_b.wait()
     own_m.wait()
 
-    def z_copies(side, t, zz):
-        at = y * NZ + zz
-        to = sides[side][0]
-        b = rows_of(ball, at * TOK, TOK)
-        return (
-            remote(b, b, zb_send.at[side, t], zb_recv.at[side, t], expert=to),
-            remote(mall.at[at], mall.at[at], zm_send.at[side, t], zm_recv.at[side, t], expert=to),
-        )
-
-    def y_copies(way, col, zz):
-        at = col * NZ + zz
-        b = rows_of(ball, at * TOK, TOK)
-        return (
-            remote(b, b, yb_send.at[way, zz], yb_recv.at[way, zz], expert=peers[way]),
-            remote(mall.at[at], mall.at[at], ym_send.at[way, zz], ym_recv.at[way, zz], expert=peers[way]),
-        )
+    def half(at, h):
+        return rows_of(ball, at * TOK + h * HALF, HALF)
+
+    def z_half(side, t, zz, h):
+        b = half(y * NZ + zz, h)
+        return remote(b, b, zb_send.at[side, t, h], zb_recv.at[side, t, h], expert=sides[side][0])
+
+    def z_meta(side, t, zz):
+        m = mall.at[y * NZ + zz]
+        return remote(m, m, zm_send.at[side, t], zm_recv.at[side, t], expert=sides[side][0])
+
+    def y_half(way, col, zz, h):
+        b = half(col * NZ + zz, h)
+        return remote(b, b, yb_send.at[way, zz, h], yb_recv.at[way, zz, h], expert=peers[way])
+
+    def y_meta(way, col, zz):
+        m = mall.at[col * NZ + zz]
+        return remote(m, m, ym_send.at[way, zz], ym_recv.at[way, zz], expert=peers[way])
 
     def far_copy(way, col, zz):
         b = rows_of(ball, (col * NZ + zz) * TOK + way * HALF, HALF)
@@ -110,25 +122,29 @@
     came_up, came_down, far = (y + NY - 1) % NY, (y + 1) % NY, (y + 2) % NY
 
     def along(t, carry):
-        for side in (0, 1):
-            zz = z + t if side else z - t
-            inside = (zz >= 0) & (zz < NZ)
-
-            @pl.when(inside & (t > 0))
-            def _():
-                for c in z_copies(side, t - 1, zz):
-                    c.wait_recv()
-
-            @pl.when(inside & sides[side][1])
-            def _():
-                for c in z_copies(side, t, zz):
-                    c.start()
-
-            @pl.when(inside & ((t > 0) if side else (t >= 0)))
-            def _():
-                for way in (0, 1):
-                    for c in y_copies(way, y, zz):
-                        c.start()
+        for h in (0, 1):
+            for side in (0, 1):
+                zz = z + t if side else z - t
+                inside = (zz >= 0) & (zz < NZ)
+
+                @pl.when(inside & (t > 0))
+                def _():
+                    if h == 0:
+                        z_meta(side, t - 1, zz).wait_recv()
+                    z_half(side, t - 1, zz, h).wait_recv()
+
+                @pl.when(inside & sides[side][1])
+                def _():
+                    if h == 0:
+                        z_meta(side, t, zz).start()
+                    z_half(side, t, zz, h).start()
+
+                @pl.when(inside & ((t > 0) if side else (t >= 0)))
+                def _():
+                    for way in (0, 1):
+                        if h == 0:
+                            y_meta(way, y, zz).start()
+                        y_half(way, y, zz, h).start()
 
         return carry
 
@@ -140,14 +156,19 @@
 
             @pl.when((zz >= 0) & (zz < NZ) & ((t > 0) if side else (t >= 0)))
             def _():
-                for c in y_copies(0, came_up, zz):
-                    c.wait_recv()
+                y_meta(0, came_up, zz).wait_recv()
+                far_meta(came_up, zz).start()
+                y_half(0, came_up, zz, 0).wait_recv()
                 far_copy(0, came_up, zz).start()
-                far_meta(came_up, zz).start()
-                for c in y_copies(1, came_down, zz):
-                    c.wait_recv()
+                y_half(1, came_down, zz, 1).wait_recv()
                 far_copy(1, came_down, zz).start()
 
+        return carry
+
+    def round_rest(zz, carry):
+        y_half(0, came_up, zz, 1).wait_recv()
+        y_meta(1, came_down, zz).wait_recv()
+        y_half(1, came_down, zz, 0).wait_recv()
         return carry
 
     def round_far(zz, carry):
@@ -197,30 +218,35 @@
         part[rows, 512:768] = jnp.dot(gr, wd[...], preferred_element_type=jnp.float32)
 
     def piece(g, o):
-        if g < NY:
-            return pl.ds(pl.multiple_of(column(g) * ROWS + o * PIECE, 16), PIECE)
-        return pl.ds(pl.multiple_of(o * ROWS + NR * PIECE, 16), REST)
-
-    def out_of(g):
-        return (snd.at[g], rcv.at[g]) if g < NY else (snd_rest, rcv_rest)
+        if g == NY:
+            return pl.ds(pl.multiple_of(o * ROWS + NR * PIECE, 16), REST)
+        c, at, size = GROUPS[g]
+        return pl.ds(pl.multiple_of(column(c) * ROWS + o * PIECE + at, 16), size)
+
+    def out_of(g, d, s):
+        if g == NY:
+            return snd_rest.at[d, s], rcv_rest.at[d, s]
+        c, at, size = GROUPS[g]
+        return snd.at[c, d, s, at:at + size], rcv.at[c, d, s, at:at + size]
 
     def rs_copy(g, d, s):
-        a, b = out_of(g)
-        return remote(a.at[d, s], b.at[d, s], rs_send.at[g, d, s], rs_recv.at[g, d, s], replica=rings[d])
+        a, b = out_of(g, d, s)
+        return remote(a, b, rs_send.at[g, d, s], rs_recv.at[g, d, s], replica=rings[d])
 
     def stage(g, s):
         for d in (0, 1):
             o = (r + NR - 1 - s) % NR if d == 0 else (r + 1 + s) % NR
             rows = piece(g, o)
-            a, b = out_of(g)
+            a = out_of(g, d, s)[0]
             if s:
+                b = out_of(g, d, s - 1)[1]
                 rs_copy(g, d, s - 1).wait_recv()
             for kind in range(3):
                 mine = part[rows, 256 * kind + 128 * d:256 * kind + 128 * d + 128]
                 cols = slice(128 * kind, 128 * kind + 128)
                 if s:
-                    mine = mine + b[d, s - 1, :, cols].astype(jnp.float32)
-                a[d, s, :, cols] = mine.astype(jnp.bfloat16)
+                    mine = mine + b[:, cols].astype(jnp.float32)
+                a[:, cols] = mine.astype(jnp.bfloat16)
             rs_copy(g, d, s).start()
 
     def ag_copy(g, d, s):
@@ -235,10 +261,10 @@
         for d in (0, 1):
             rs_copy(g, d, 2).wait_recv()
             rows = piece(g, r)
-            b = out_of(g)[1]
+            b = out_of(g, d, 2)[1]
             gate, upp, dh = [
                 part[rows, 256 * kind + 128 * d:256 * kind + 128 * d + 128]
-                + b[d, 2, :, 128 * kind:128 * kind + 128].astype(jnp.float32)
+                + b[:, 128 * kind:128 * kind + 128].astype(jnp.float32)
                 for kind in range(3)
             ]
             sg = jax.nn.sigmoid(gate)
@@ -287,22 +313,26 @@
 
     products(0)
     stage(0, 0)
-    for d in (0, 1):
-        wcat[d, :, 0:128] = wg[:, 128 * d:128 * d + 128]
-        wcat[d, :, 128:256] = wu[:, 128 * d:128 * d + 128]
+    stage(5, 0)
     lax.fori_loop(0, NZ, round_y, 0)
+    lax.fori_loop(0, NZ, round_rest, 0)
     stage(0, 1)
+    stage(5, 1)
     products(1)
     stage(1, 0)
     products(2)
     stage(2, 0)
     stage(0, 2)
+    stage(5, 2)
     lax.fori_loop(0, NZ, round_far, 0)
     products(3)
     stage(4, 0)
     stage(3, 0)
     for g in (1, 2, 4, 3):
         stage(g, 1)
+    for d in (0, 1):
+        wcat[d, :, 0:128] = wg[:, 128 * d:128 * d + 128]
+        wcat[d, :, 128:256] = wu[:, 128 * d:128 * d + 128]
     for g in range(NY):
         choose(picks.at[g], 0, y, (y + (0, 3, 1, 2)[g]) % NY * 2 + z // SHARES)
     for g in (1, 2, 4, 3):
@@ -316,25 +346,29 @@
     onward(4, 1)
     onward(1, 2)
     final(0)
+    final(5)
     onward(3, 1)
     onward(2, 2)
     onward(4, 2)
+    onward(1, 3)
+    onward(0, 1)
+    onward(5, 1)
+    onward(3, 2)
+    onward(2, 3)
     onward(4, 3)
-    onward(1, 3)
     backward(1)
-    onward(3, 2)
-    onward(0, 1)
-    weights(1, True)
-    onward(2, 3)
     backward(2)
     onward(0, 2)
-    weights(2, False)
+    onward(5, 2)
+    weights(1, True)
     onward(3, 3)
     backward(3)
+    weights(2, False)
     weights(3, False)
     collect(1, True)
     collect(2, False)
     onward(0, 3)
+    onward(5, 3)
     backward(0)
     collect(0, False)
     collect(3, False)
@@ -376,7 +410,18 @@
                 z_copy(side, h, z).wait_recv()
                 total[at, :] = total[at, :] + zrcv[side, h, z].astype(jnp.float32)
 
-        o_ref[h * HALF:h * HALF + HALF, :] = total[at, :].astype(jnp.bfloat16)
+        edge[h * HALF:h * HALF + HALF, :] = total[at, :].astype(jnp.bfloat16)
+
+    def shift():
+        return remote(edge, o_ref, s_send, s_recv, section=sec - 1)
+
+    @pl.when(sec > 0)
+    def _():
+        shift().start()
+
+    @pl.when(sec == NS - 1)
+    def _():
+        o_ref[...] = jnp.zeros_like(o_ref)
 
     for d in (0, 1):
         cols = slice(128 * d, 128 * d + 128)
@@ -387,16 +432,18 @@
     def finish(zz, carry):
         for way in (0, 1):
             far_copy(way, (came_up, came_down)[way], zz).wait_send()
-            for c in y_copies(way, y, zz):
-                c.wait_send()
+            y_meta(way, y, zz).wait_send()
+            for h in (0, 1):
+                y_half(way, y, zz, h).wait_send()
         far_meta(came_up, zz).wait_send()
         for side in (0, 1):
             src = z + zz if side else z - zz
 
             @pl.when((src >= 0) & (src < NZ) & sides[side][1])
             def _():
-                for c in z_copies(side, zz, src):
-                    c.wait_send()
+                z_meta(side, zz, src).wait_send()
+                for h in (0, 1):
+                    z_half(side, zz, src, h).wait_send()
 
         for h in (0, 1):
             @pl.when(zz > z)
@@ -410,13 +457,21 @@
         return carry
 
     lax.fori_loop(0, NZ, finish, 0)
-    for g in range(NY + 1):
+    for g in range(len(GROUPS)):
         for d in (0, 1):
             for s in range(NR - 1):
                 rs_copy(g, d, s).wait_send()
                 ag_copy(g, d, s).wait_send()
     for g in (1, 2, 3):
         back_copy(g).wait_send()
+
+    @pl.when(sec > 0)
+    def _():
+        shift().wait_send()
+
+    @pl.when(sec < NS - 1)
+    def _():
+        shift().wait_recv()
 
 
 def layer(tokens, meta, wg, wu, wd):
@@ -438,19 +493,13 @@
             vm((2, rows, 384), bf), vm((2, D, 256), bf), vm((2, D, 384), f32),
             vm((NY, ROWS, D), bf), vm((NY, ROWS, D), bf), vm((TOKS, D), f32),
             vm((2, 2, NZ, HALF, D), bf), vm((2, 2, NZ, HALF, D), bf),
-            dma((2,)),
-        ] + [dma((2, NZ))] * 10 + [dma((NZ,))] * 2 + [dma((NY + 1, 2, 3))] * 4
-        + [dma((NY,))] * 2 + [dma((2, 2, NZ))] * 2,
+            vm((TOK, D), bf), dma((2,)),
+        ] + ([dma((2, NZ, 2))] * 2 + [dma((2, NZ))] * 2) * 2 + [dma((2, NZ))] * 2 + [dma((NZ,))] * 2
+        + [dma((len(GROUPS), 2, 3))] * 4 + [dma((NY,))] * 2 + [dma((2, 2, NZ))] * 2 + [dma(()), dma(())],
         compiler_params=pltpu.CompilerParams(
             collective_id=0, has_side_effects=True, vmem_limit_bytes=VMEM_LIMIT
         ),
     )(tokens, meta, wg, wu, wd)
-
-
-def shifted(value, axis, steps):
-    count = lax.axis_size(axis)
-    first, last = (max(0, -steps), min(count, count - steps))
-    return lax.ppermute(value, axis, [(source, source + steps) for source in range(first, last)])
 
 
 def table_of(routes, weights):
@@ -467,9 +516,8 @@
 def per_device(token_grads, routing, gate_weights, layer_inputs, w_gate, w_up, w_down):
     block = jnp.concatenate([layer_inputs[0], token_grads[0]], axis=1)
     meta = table_of(routing[0], gate_weights[0])
-    boundary, grad_gate, grad_up, grad_down = layer(block, meta, w_gate[0], w_up[0], w_down[0])
-    upstream = shifted(boundary[None], "section", -1)
-    return (upstream, grad_gate[None], grad_up[None], grad_down[None])
+    upstream, grad_gate, grad_up, grad_down = layer(block, meta, w_gate[0], w_up[0], w_down[0])
+    return (upstream[None], grad_gate[None], grad_up[None], grad_down[None])
 
 
 def solution(mesh):

time: 364 us -> 362 us (level)
  the two profiles are of different devices: /device:TPU:5 before, /device:TPU:43 now
where the time goes in v3:
time: 362 us; the launch traced here: 361 us
  Pallas kernels  352 us (97%)
  local copies, waits for them, and re-layouts  6.06 us (2%)
    pallas_call x1, Pallas kernels, layer(): pl.pallas_call(kernel, out_shape=(jax.ShapeDtypeStruct((TOK, D), bf),) +...  352 us

profile of v3, /device:TPU:43, one launch (start us, length us, event | category | flops | bytes accessed | tf_op | source)
XLA Modules:
  0.0 361.4 jit_solution(4889861076171248512)
XLA Ops:
  0.6 0.0 copy-start.3
  0.6 0.0 copy-start.2
  0.7 0.7 copy-done.3
  1.3 0.0 copy-done.2
  1.3 0.1 convolution_select_fusion
  1.5 0.7 maximum_maximum_fusion.m_ref
  2.1 1.7 pad_maximum_fusion.b_ref
  3.8 352.2 %shard_map.102 = (bf16[64,896]{1,0:T(8,128)(2,1)}, bf16[896,256]{1,0:T(8,128)(2,1)}, bf16[896,256]{1,0:T(8,128)(2,1)}, bf16[896,256]{1,0:T(8,128)(2,1)}) custom-call(bf16[64,1792]{1,0:T(8,128)(2,1)} %pad_maximum_fusion.b_ref, f32[16,128]{1,0:T(8,128)} %maximum_maximum_fusion.m_ref, bf16[896,256]{1,0:T(8,128)(2,1)} %bitcast.18, bf16[896,256]{1,0:T(8,128)(2,1)} %bitcast.19, ...), custom_call_target="tpu_custom_call" | custom-call | tf_op jit(solution)/shard_map/pallas_call | solution.py:482
  356.0 1.6 copy.15
  357.6 0.0 copy-start.1
  357.6 1.9 copy.16
  359.5 0.0 copy-done.1
  359.5 0.0 copy-start
  359.5 0.8 copy.17
  360.2 0.4 copy-done
  360.6 0.8 copy.18
  (1 shorter events, 0.0 us)
Async XLA Ops:
  0.6 0.7 copy-start.3
  0.6 0.7 copy-start.2
  357.6 1.9 copy-start.1
  359.5 1.2 copy-start

commit v4 on v3

--- a/solution.py
+++ b/solution.py
@@ -295,15 +295,15 @@
 
     def weights(g, fresh):
         rows = column_rows(g)
-        for d in (0, 1):
-            up_down = over_rows(xs[rows, :], act[d, rows, 128:384])
-            hid = over_rows(gs[rows, :], act[d, rows, 0:128])
-            if fresh:
-                gacc[d, :, 128:384] = up_down
-                gacc[d, :, 0:128] = hid
-            else:
-                gacc[d, :, 128:384] = gacc[d, :, 128:384] + up_down
-                gacc[d, :, 0:128] = gacc[d, :, 0:128] + hid
+        both = jnp.concatenate([act[0, rows, 128:384], act[1, rows, 128:384]], axis=1)
+        up_down = over_rows(xs[rows, :], both)
+        hid = over_rows(gs[rows, :], jnp.concatenate([act[0, rows, 0:128], act[1, rows, 0:128]], axis=1))
+        if fresh:
+            gacc[:, 0:512] = up_down
+            gacc[:, 512:768] = hid
+        else:
+            gacc[:, 0:512] = gacc[:, 0:512] + up_down
+            gacc[:, 512:768] = gacc[:, 512:768] + hid
 
     def collect(g, fresh):
         if g:
@@ -340,38 +340,37 @@
     final(1)
     final(2)
     final(4)
+    final(0)
+    final(5)
     onward(1, 1)
     final(3)
+    onward(4, 1)
     onward(2, 1)
-    onward(4, 1)
     onward(1, 2)
-    final(0)
-    final(5)
     onward(3, 1)
-    onward(2, 2)
+    onward(0, 1)
+    onward(5, 1)
     onward(4, 2)
     onward(1, 3)
-    onward(0, 1)
-    onward(5, 1)
     onward(3, 2)
-    onward(2, 3)
+    onward(2, 2)
     onward(4, 3)
     backward(1)
-    backward(2)
+    onward(3, 3)
+    backward(3)
     onward(0, 2)
     onward(5, 2)
+    onward(2, 3)
+    backward(2)
     weights(1, True)
-    onward(3, 3)
-    backward(3)
-    weights(2, False)
     weights(3, False)
     collect(1, True)
+    collect(3, False)
     collect(2, False)
     onward(0, 3)
     onward(5, 3)
     backward(0)
     collect(0, False)
-    collect(3, False)
 
     def z_copy(side, h, zz):
         return remote(zsnd.at[side, h, zz], zrcv.at[side, h, zz],
@@ -400,6 +399,7 @@
         return carry
 
     lax.fori_loop(0, 1, slot, 0)
+    weights(2, False)
     weights(0, False)
     lax.fori_loop(1, NZ - 1, slot, 0)
     for h in (0, 1):
@@ -425,9 +425,9 @@
 
     for d in (0, 1):
         cols = slice(128 * d, 128 * d + 128)
-        gd[:, cols] = gacc[d, :, 0:128].astype(jnp.bfloat16)
-        gg[:, cols] = gacc[d, :, 128:256].astype(jnp.bfloat16)
-        gu[:, cols] = gacc[d, :, 256:384].astype(jnp.bfloat16)
+        gg[:, cols] = gacc[:, 256 * d:256 * d + 128].astype(jnp.bfloat16)
+        gu[:, cols] = gacc[:, 256 * d + 128:256 * d + 256].astype(jnp.bfloat16)
+        gd[:, cols] = gacc[:, 512 + 128 * d:640 + 128 * d].astype(jnp.bfloat16)
 
     def finish(zz, carry):
         for way in (0, 1):
@@ -490,7 +490,7 @@
             vm((rows, D), bf), vm((rows, D), bf), vm((rows, 3 * H), f32),
             vm((NY, 2, 3, PIECE, 384), bf), vm((NY, 2, 3, PIECE, 384), bf),
             vm((2, 3, REST, 384), bf), vm((2, 3, REST, 384), bf),
-            vm((2, rows, 384), bf), vm((2, D, 256), bf), vm((2, D, 384), f32),
+            vm((2, rows, 384), bf), vm((2, D, 256), bf), vm((D, 768), f32),
             vm((NY, ROWS, D), bf), vm((NY, ROWS, D), bf), vm((TOKS, D), f32),
             vm((2, 2, NZ, HALF, D), bf), vm((2, 2, NZ, HALF, D), bf),
             vm((TOK, D), bf), dma((2,)),

time: 362 us -> 360 us (level)
  the two profiles are of different devices: /device:TPU:43 before, /device:TPU:51 now
where the time goes in v4:
time: 360 us; the launch traced here: 359 us
  Pallas kernels  350 us (97%)
  local copies, waits for them, and re-layouts  6.06 us (2%)
    pallas_call x1, Pallas kernels, layer(): pl.pallas_call(kernel, out_shape=(jax.ShapeDtypeStruct((TOK, D), bf),) +...  350 us

profile of v4, /device:TPU:51, one launch (start us, length us, event | category | flops | bytes accessed | tf_op | source)
XLA Modules:
  0.0 359.3 jit_solution(11413721825639301972)
XLA Ops:
  0.6 0.0 copy-start.3
  0.6 0.0 copy-start.2
  0.7 0.7 copy-done.3
  1.3 0.0 copy-done.2
  1.3 0.1 convolution_select_fusion
  1.5 0.7 maximum_maximum_fusion.m_ref
  2.1 1.7 pad_maximum_fusion.b_ref
  3.8 350.1 %shard_map.102 = (bf16[64,896]{1,0:T(8,128)(2,1)}, bf16[896,256]{1,0:T(8,128)(2,1)}, bf16[896,256]{1,0:T(8,128)(2,1)}, bf16[896,256]{1,0:T(8,128)(2,1)}) custom-call(bf16[64,1792]{1,0:T(8,128)(2,1)} %pad_maximum_fusion.b_ref, f32[16,128]{1,0:T(8,128)} %maximum_maximum_fusion.m_ref, bf16[896,256]{1,0:T(8,128)(2,1)} %bitcast.18, bf16[896,256]{1,0:T(8,128)(2,1)} %bitcast.19, ...), custom_call_target="tpu_custom_call" | custom-call | tf_op jit(solution)/shard_map/pallas_call | solution.py:482
  353.9 1.6 copy.15
  355.5 0.0 copy-start.1
  355.5 1.9 copy.16
  357.4 0.0 copy-done.1
  357.4 0.0 copy-start
  357.4 0.8 copy.17
  358.1 0.4 copy-done
  358.6 0.8 copy.18
  (1 shorter events, 0.0 us)
Async XLA Ops:
  0.6 0.7 copy-start.3
  0.6 0.7 copy-start.2
  355.5 1.9 copy-start.1
  357.4 1.2 copy-start
